TPU v7x, 256 devices: a whole 4x4x8 slice. The times are simulated.
256 devices in a mesh: group: 16 (over y, x), member: 16 (over z, core).
Axes of the slice: x: 4, y: 4, z: 8, core: 2. Of those that a mesh axis runs over, the one named last changes fastest.
Arguments:
- factor: float32 [16, 32, 768, 768], P('group', 'member'), as said below
- load: float32 [16, 32, 768], P('group', 'member'), may hold values from -6 to 6
- dof_map: int32 [16, 32, 768], P('group', 'member'), may hold values from 0 to 767, as said below
- dof_sign: int32 [16, 32, 768], P('group', 'member'), may hold values from -1 to 1, as said below
- live_count: int32 [16, 32], P('group', 'member'), may hold values from 384 to 768, as said below
- face_slot: int32 [16, 32, 4, 64], P('group', 'member'), may hold values from 0 to 767, as said below
- face_count: int32 [16, 32, 4], P('group', 'member'), may hold values from 0 to 64, as said below
- node_coord: int32 [16, 32, 3, 256], P('group', 'member'), may hold values from 0 to 15
- coarse_inverse: float32 [3072, 3072], P(('group', 'member')), as said below
Outputs:
- multipliers: float32 [16, 32, 768], P('group', 'member')
- projected: float32 [16, 32, 768], P('group', 'member')
Inputs may be any that keep to these rules, and one draw needn't show every extreme that they name: `dof_map`: each subdomain's row is a permutation of the unknowns. `dof_sign`: every entry is -1 or 1. `live_count`: in each cluster, both subdomains of one device have 768 live multipliers and both subdomains of the device whose member index differs by a quarter of 32 have 384. `face_slot`: the slots of one subdomain are distinct and below its live_count; slot k of a face pairs with slot k of the partner's face. `face_count`: A face and its partner's face have the same count; faces at the ends of a cluster's chain and at the first and last cluster have 0, all others 1 or more. `factor`: lower triangular with a positive diagonal. `coarse_inverse`: symmetric positive definite.
All inputs are finite; a program needn't handle non-finite values.
Results may differ from a plain program's by a relative error of at most 0.0003.
Values sent between devices are 32-bit elements; how exact they have to be, the bound alone decides.
No kernel may reach another device: no remote copies, remote signals or barrier semaphores. Data moves between devices by JAX's collectives and lax.ppermute only.
A program may use at most 128 MiB of HBM per device.

v0:
```python
import math
import jax
import jax.numpy as jnp
from jax import lax
from jax.sharding import PartitionSpec as P

ITERS = 3
highest = lax.Precision.HIGHEST
half_span = 8.0


def from_partner(value, axis, bit):
    mask = 2**bit
    pairs = [(source, source ^ mask) for source in range(lax.axis_size(axis))]
    return lax.ppermute(value, axis, pairs)


def padded(array, sides, width):
    for axis, dim in sides:
        size, length = (lax.axis_size(axis), array.shape[dim])
        up = [(i, (i + 1) % size) for i in range(size - 1)]
        down = [(j, i) for i, j in up]
        last = lax.slice_in_dim(array, length - width, length, axis=dim)
        leading = lax.slice_in_dim(array, 0, width, axis=dim)
        before = lax.ppermute(last, axis, up)
        after = lax.ppermute(leading, axis, down)
        array = jnp.concatenate([before, array, after], axis=dim)
    return array


def rigid_modes(node_coord):
    position = (node_coord.astype(jnp.float32) - half_span) / half_span
    spread = jnp.repeat(position, 3, axis=-1)
    component = jnp.arange(spread.shape[-1], dtype=jnp.int32) % 3
    first = (component == 0).astype(spread.dtype)
    second = (component == 1).astype(spread.dtype)
    third = (component == 2).astype(spread.dtype)
    coord_x = spread[..., 0, :]
    coord_y = spread[..., 1, :]
    coord_z = spread[..., 2, :]
    unit_row = jnp.ones_like(coord_x)
    return jnp.stack(
        [
            first * unit_row,
            second * unit_row,
            third * unit_row,
            third * coord_y - second * coord_z,
            first * coord_z - third * coord_x,
            second * coord_x - first * coord_y,
        ],
        axis=-2,
    )


def lower_solve(panel_matrix, right_side):
    return lax.linalg.triangular_solve(panel_matrix, right_side, left_side=True, lower=True)


def upper_solve(panel_matrix, right_side):
    return lax.linalg.triangular_solve(
        panel_matrix, right_side, left_side=True, lower=True, transpose_a=True
    )


def dual_of(panel_matrix, dof_codes, block_count, block_width):
    dof_count = panel_matrix.shape[0]
    slot_total = dof_codes.shape[0]
    levels = jnp.arange(dof_count, dtype=jnp.float32)[:, None]

    def solve_block(block_index, solved):
        columns = lax.dynamic_slice_in_dim(dof_codes, block_index * block_width, block_width)
        target = jnp.where(
            levels == jnp.abs(columns)[None, :] - 1.0, jnp.sign(columns)[None, :], 0.0
        )
        solved_piece = lower_solve(panel_matrix, target)
        return lax.dynamic_update_slice_in_dim(solved, solved_piece, block_index * block_width, 1)

    solved = lax.fori_loop(
        0, block_count, solve_block, jnp.zeros((dof_count, slot_total), jnp.float32)
    )

    def product_block(block_index, dual_sum):
        solved_piece = lax.dynamic_slice_in_dim(solved, block_index * block_width, block_width, 1)
        column = lax.dot_general(
            solved,
            solved_piece,
            (((0,), (0,)), ((), ())),
            precision=highest,
            preferred_element_type=jnp.float32,
        )
        return lax.dynamic_update_slice_in_dim(dual_sum, column, block_index * block_width, 1)

    return lax.fori_loop(
        0, block_count, product_block, jnp.zeros((slot_total, slot_total), jnp.float32)
    )


def shards(
    factor, load, dof_map, dof_sign, live_count, face_slot, face_count, node_coord, coarse_inverse
):
    own_panels = factor[0]
    own_loads = load[0]
    dof_count = own_loads.shape[1]
    subs_here = own_loads.shape[0]
    face_cap = face_slot.shape[3]
    block_width = math.gcd(dof_count, 128)
    positions = jnp.arange(dof_count, dtype=jnp.int32)
    live_mask = positions[None, :] < live_count[0][:, None]
    signed = jnp.where(live_mask, dof_sign[0], 0)
    dof_codes = ((dof_map[0] + 1) * signed).astype(jnp.float32)
    signed_float = signed.astype(jnp.float32)
    blocks_own = (live_count[0] + block_width - 1) // block_width
    bit_pos = lax.axis_size("member").bit_length() - 2
    partner_panel, partner_codes = from_partner((own_panels[1], dof_codes), "member", bit_pos)
    first_dual = dual_of(own_panels[0], dof_codes[0], blocks_own[0], block_width)
    partner_blocks = (
        jnp.sum((partner_codes != 0).astype(jnp.int32), axis=1) + block_width - 1
    ) // block_width
    upper_half = lax.axis_index("member") // (lax.axis_size("member") // 2) % 2 == 1
    lower_blocks = jnp.where(upper_half, partner_blocks, blocks_own)
    upper_blocks = jnp.where(upper_half, blocks_own, partner_blocks)
    lower_loads = jnp.stack(
        [
            lower_blocks[0] + lower_blocks[1],
            lower_blocks[0],
            lower_blocks[0] + lower_blocks[1] + upper_blocks[1],
            lower_blocks[0] + upper_blocks[1],
        ]
    )
    upper_loads = jnp.stack(
        [
            upper_blocks[0] + upper_blocks[1],
            upper_blocks[0] + upper_blocks[1] + lower_blocks[1],
            upper_blocks[0],
            upper_blocks[0] + lower_blocks[1],
        ]
    )
    option_pick = jnp.argmin(jnp.maximum(lower_loads, upper_loads))
    lower_moves = (option_pick == 1) | (option_pick == 3)
    upper_moves = (option_pick == 2) | (option_pick == 3)
    give_mine = jnp.where(upper_half, upper_moves, lower_moves)
    take_theirs = jnp.where(upper_half, lower_moves, upper_moves)
    kept_dual = dual_of(
        own_panels[1], dof_codes[1], jnp.where(give_mine, 0, blocks_own[1]), block_width
    )
    helped_dual = dual_of(
        partner_panel, partner_codes[1], jnp.where(take_theirs, partner_blocks[1], 0), block_width
    )
    returned = from_partner(helped_dual, "member", bit_pos)
    second_dual = jnp.where(give_mine, returned, kept_dual)
    dual_pair = jnp.stack([first_dual, second_dual])
    forward = jax.vmap(lambda panel_one, load_one: lower_solve(panel_one, load_one[:, None]))(
        own_panels, own_loads
    )
    displaced = jax.vmap(upper_solve)(own_panels, forward)[:, :, 0]
    gap_local = jnp.take_along_axis(displaced, dof_map[0], axis=1) * signed_float
    mode_table = rigid_modes(node_coord[0])
    rigid_rows = jnp.take_along_axis(
        mode_table, jnp.broadcast_to(dof_map[0][:, None, :], mode_table.shape), axis=2
    )
    rigid_rows = rigid_rows * signed_float[:, None, :]
    coarse_rhs = jnp.einsum("lai,li->la", mode_table, own_loads, precision=highest)
    slot_list = face_slot[0].reshape(subs_here, 4 * face_cap)
    slot_used = (
        jnp.arange(face_cap, dtype=jnp.int32)[None, None, :] < face_count[0][:, :, None]
    ).reshape(subs_here, 4 * face_cap)
    slot_table = (
        (slot_list[:, :, None] == positions[None, None, :]) & slot_used[:, :, None]
    ).astype(jnp.float32)
    shared = jnp.sum(slot_table, axis=1)
    weight = live_mask.astype(jnp.float32) * (1.0 - 0.5 * shared)

    def assemble(values):
        outgoing = jnp.einsum("lkj,lj->lk", slot_table, values, precision=highest)
        extended = padded(outgoing[None], (("group", 0), ("member", 1)), 1)
        incoming = jnp.stack(
            [
                jnp.concatenate(
                    [
                        extended[1, sub_index, face_cap : 2 * face_cap],
                        extended[1, sub_index + 2, 0:face_cap],
                        extended[0, sub_index + 1, 3 * face_cap : 4 * face_cap],
                        extended[2, sub_index + 1, 2 * face_cap : 3 * face_cap],
                    ]
                )
                for sub_index in range(subs_here)
            ]
        )
        return values + jnp.einsum("lk,lkj->lj", incoming, slot_table, precision=highest)

    def inner_part(left_field, right_field):
        return jnp.sum(weight * left_field * right_field)

    def global_sum(partial_value):
        return lax.psum(partial_value, ("group", "member"))

    def gather_coarse(local_coarse):
        return lax.all_gather(local_coarse.reshape(1, -1), ("group", "member"), axis=0, tiled=True)

    def coarse_of(values):
        return jnp.einsum("laj,lj->la", rigid_rows, values, precision=highest)

    def spread_modes(gathered):
        alpha = jnp.dot(coarse_inverse, gathered.reshape(-1), precision=highest).reshape(
            subs_here, -1
        )
        return assemble(jnp.einsum("laj,la->lj", rigid_rows, alpha, precision=highest))

    def apply_dual(values):
        return jnp.einsum("lij,lj->li", dual_pair, values, precision=highest)

    multipliers = spread_modes(gather_coarse(coarse_rhs))
    residual = assemble(gap_local - apply_dual(multipliers))
    coarse_res = gather_coarse(coarse_of(residual))
    projected = residual - spread_modes(coarse_res)
    direction = projected
    norm_now = global_sum(inner_part(projected, projected))
    for iteration in range(ITERS):
        image_vec = assemble(apply_dual(direction))
        curvature = global_sum(inner_part(direction, image_vec))
        step_size = norm_now / curvature
        multipliers = multipliers + step_size * direction
        residual = residual - step_size * image_vec
        coarse_res = gather_coarse(coarse_of(residual))
        projected = residual - spread_modes(coarse_res)
        norm_next = global_sum(inner_part(projected, projected))
        direction = projected + norm_next / norm_now * direction
        norm_now = norm_next
    return (multipliers[None], projected[None])


def solution(mesh):
    return jax.shard_map(
        shards,
        mesh=mesh,
        in_specs=(
            P("group", "member", None, None),
            P("group", "member", None),
            P("group", "member", None),
            P("group", "member", None),
            P("group", "member"),
            P("group", "member", None, None),
            P("group", "member", None),
            P("group", "member", None, None),
            P(("group", "member"), None),
        ),
        out_specs=(P("group", "member", None), P("group", "member", None)),
        check_vma=False,
    )
```

profile of v0, /device:TPU:15, one launch (start us, length us, event | category | flops | bytes accessed | tf_op | source)
XLA Modules:
  0.0 2192.2 jit_solution(2142416162315321795)
XLA Ops:
  4.6 71.1 %gather_fusion = f32[9216]{0:T(1024)S(1)} fusion(f32[2,6,768]{2,1,0:T(8,128)S(1)} %stack.144, s32[9216]{0:T(1024)S(1)} %reshape.418), kind=kCustom, calls=%fused_computation | custom fusion | bytes 184320 | tf_op jit(solution)/shard_map/jit(take_along_axis)/gather | solution.py:158
  75.9 58.2 %all-gather = f32[256,1,12]{2,1,0:T(1,128)S(1)} all-gather(f32[1,1,12]{2,1,0:T(1,128)S(1)} %reshape.430), channel_id=1, replica_groups=mesh['group'=16,'member'=16] {'group','member'}, dimensions={0}, use_global_device_ids=true | all-gather | bytes 12336 | tf_op jit(solution)/shard_map/all_gather | solution.py:198
  179.9 117.9 %custom-call.8 = f32[2,6,128,128]{2,3,1,0:T(8,128)S(1)} custom-call(f32[2,6,128,128]{3,2,1,0:T(8,128)S(1)} %bitcast.1018), custom_call_target="InvertDiagBlocksLowerTriangular" | custom-call | tf_op jit(solution)/shard_map/vmap()/triangular_solve | solution.py:60
  351.9 324.7 %while.88 = (s32[]{:T(128)}, f32[768,768]{1,0:T(8,128)}, s32[]{:T(128)}, f32[768]{0:T(1024)S(1)}, f32[768,768]{1,0:T(8,128)}, /*index=5*/s32[]{:T(128)}, s32[]{:T(128)}, s32[]{:T(128)}, s32[]{:T(128)}, s32[]{:T(128)}) while((s32[]{:T(128)}, f32[768,768]{1,0:T(8,128)}, s32[]{:T(128)}, f32[768]{0:T(1024)S(1)}, ...), condition=%wide.region_12.14_spmd.clone, body=%wide.region_11.13_spmd.clone.sunk | while | flops 530268544 | bytes 10424716 | solution.py:78
  369.2 59.8 %custom-call.57 = f32[6,128,128]{1,2,0:T(8,128)S(1)} custom-call(f32[6,128,128]{2,1,0:T(8,128)} %get-tuple-element.1070), custom_call_target="InvertDiagBlocksLowerTriangular" | custom-call | tf_op jit(solution)/shard_map/while/body/triangular_solve/custom-call.1 | solution.py:56
  450.3 59.8 %custom-call.57 = f32[6,128,128]{1,2,0:T(8,128)S(1)} custom-call(f32[6,128,128]{2,1,0:T(8,128)} %get-tuple-element.1070), custom_call_target="InvertDiagBlocksLowerTriangular" | custom-call | tf_op jit(solution)/shard_map/while/body/triangular_solve/custom-call.1 | solution.py:56
  531.4 59.8 %custom-call.57 = f32[6,128,128]{1,2,0:T(8,128)S(1)} custom-call(f32[6,128,128]{2,1,0:T(8,128)} %get-tuple-element.1070), custom_call_target="InvertDiagBlocksLowerTriangular" | custom-call | tf_op jit(solution)/shard_map/while/body/triangular_solve/custom-call.1 | solution.py:56
  612.6 59.8 %custom-call.57 = f32[6,128,128]{1,2,0:T(8,128)S(1)} custom-call(f32[6,128,128]{2,1,0:T(8,128)} %get-tuple-element.1070), custom_call_target="InvertDiagBlocksLowerTriangular" | custom-call | tf_op jit(solution)/shard_map/while/body/triangular_solve/custom-call.1 | solution.py:56
  681.2 84.4 %collective-permute-start.6 = (f32[768,768]{0,1:T(8,128)}, f32[768,768]{0,1:T(8,128)}, u32[]{:S(2)}, u32[]{:S(2)}) collective-permute-start(f32[768,768]{0,1:T(8,128)} %get-tuple-element.317), channel_id=1, source_target_pairs={{0,8},{1,9},{2,10},{3,11},{4,12},{5,13},{6,14},{7,15},{8,0},{9,1},... | collective-permute-start | bytes 7077896 | tf_op jit(solution)/shard_map/ppermute | solution.py:15
  767.2 496.1 %while.84 = (s32[]{:T(128)}, f32[768,768]{1,0:T(8,128)}, s32[]{:T(128)}, f32[768]{0:T(1024)S(1)}, f32[768,768]{1,0:T(8,128)}, /*index=5*/s32[]{:T(128)}, s32[]{:T(128)}, s32[]{:T(128)}, s32[]{:T(128)}, s32[]{:T(128)}) while((s32[]{:T(128)}, f32[768,768]{1,0:T(8,128)}, s32[]{:T(128)}, f32[768]{0:T(1024)S(1)}, f32[768,768]{1,0:T(8,128)}, ...), condition=%wide.region_2.4_spmd.clone, body=%wide.region_1.3_spmd.clone.sunk | while | flops 530268544 | bytes 10424716 | solution.py:78
  785.8 59.8 %custom-call.51 = f32[6,128,128]{1,2,0:T(8,128)S(1)} custom-call(f32[6,128,128]{2,1,0:T(8,128)} %get-tuple-element.1024), custom_call_target="InvertDiagBlocksLowerTriangular" | custom-call | tf_op jit(solution)/shard_map/while/body/triangular_solve/custom-call.1 | solution.py:56
  868.3 59.8 %custom-call.51 = f32[6,128,128]{1,2,0:T(8,128)S(1)} custom-call(f32[6,128,128]{2,1,0:T(8,128)} %get-tuple-element.1024), custom_call_target="InvertDiagBlocksLowerTriangular" | custom-call | tf_op jit(solution)/shard_map/while/body/triangular_solve/custom-call.1 | solution.py:56
  950.9 59.8 %custom-call.51 = f32[6,128,128]{1,2,0:T(8,128)S(1)} custom-call(f32[6,128,128]{2,1,0:T(8,128)} %get-tuple-element.1024), custom_call_target="InvertDiagBlocksLowerTriangular" | custom-call | tf_op jit(solution)/shard_map/while/body/triangular_solve/custom-call.1 | solution.py:56
  1033.5 59.8 %custom-call.51 = f32[6,128,128]{1,2,0:T(8,128)S(1)} custom-call(f32[6,128,128]{2,1,0:T(8,128)} %get-tuple-element.1024), custom_call_target="InvertDiagBlocksLowerTriangular" | custom-call | tf_op jit(solution)/shard_map/while/body/triangular_solve/custom-call.1 | solution.py:56
  1116.1 59.8 %custom-call.51 = f32[6,128,128]{1,2,0:T(8,128)S(1)} custom-call(f32[6,128,128]{2,1,0:T(8,128)} %get-tuple-element.1024), custom_call_target="InvertDiagBlocksLowerTriangular" | custom-call | tf_op jit(solution)/shard_map/while/body/triangular_solve/custom-call.1 | solution.py:56
  1198.6 59.8 %custom-call.51 = f32[6,128,128]{1,2,0:T(8,128)S(1)} custom-call(f32[6,128,128]{2,1,0:T(8,128)} %get-tuple-element.1024), custom_call_target="InvertDiagBlocksLowerTriangular" | custom-call | tf_op jit(solution)/shard_map/while/body/triangular_solve/custom-call.1 | solution.py:56
  1332.9 142.5 %all-gather.1 = f32[256,1,12]{2,1,0:T(1,128)S(1)} all-gather(f32[1,1,12]{2,1,0:T(1,128)S(1)} %reshape.432), channel_id=1, replica_groups=mesh['group'=16,'member'=16] {'group','member'}, dimensions={0}, use_global_device_ids=true | all-gather | bytes 12336 | tf_op jit(solution)/shard_map/all_gather | solution.py:198
  1521.2 76.7 %all-reduce = (f32[]{:T(128)}, f32[]{:T(128)}) all-reduce(f32[]{:T(128)} %get-tuple-element.439, f32[]{:T(128)} %get-tuple-element.438), channel_id=1, replica_groups=mesh['group'=16,'member'=16] {'group','member'}, use_global_device_ids=true, to_apply=%region_16.18 | all-reduce | flops 2 | bytes 16 | tf_op jit(solution)/shard_map/psum | solution.py:195
  1678.0 74.4 %psum.44 = f32[]{:T(128)} all-reduce(f32[]{:T(128)} %fusion.217), channel_id=1, replica_groups=mesh['group'=16,'member'=16] {'group','member'}, use_global_device_ids=true, to_apply=%region_20.22 | all-reduce | flops 1 | bytes 8 | tf_op jit(solution)/shard_map/psum | solution.py:195
  1778.7 75.6 %psum.45 = f32[]{:T(128)} all-reduce(f32[]{:T(128)} %multiply_reduce_fusion.1), channel_id=1, replica_groups=mesh['group'=16,'member'=16] {'group','member'}, use_global_device_ids=true, to_apply=%region_22.24 | all-reduce | flops 1 | bytes 8 | tf_op jit(solution)/shard_map/psum | solution.py:195
  1855.9 54.4 %all-gather.3 = f32[256,1,12]{2,1,0:T(1,128)S(1)} all-gather(f32[1,1,12]{2,1,0:T(1,128)S(1)} %reshape.436), channel_id=1, replica_groups=mesh['group'=16,'member'=16] {'group','member'}, dimensions={0}, use_global_device_ids=true | all-gather | bytes 12336 | tf_op jit(solution)/shard_map/all_gather | solution.py:198
  1935.1 73.6 %psum.46 = f32[]{:T(128)} all-reduce(f32[]{:T(128)} %get-tuple-element.530), channel_id=1, replica_groups=mesh['group'=16,'member'=16] {'group','member'}, use_global_device_ids=true, to_apply=%region_24.26 | all-reduce | flops 1 | bytes 8 | tf_op jit(solution)/shard_map/psum | solution.py:195
  2035.8 74.8 %psum.47 = f32[]{:T(128)} all-reduce(f32[]{:T(128)} %multiply_reduce_fusion), channel_id=1, replica_groups=mesh['group'=16,'member'=16] {'group','member'}, use_global_device_ids=true, to_apply=%region_26.28 | all-reduce | flops 1 | bytes 8 | tf_op jit(solution)/shard_map/psum | solution.py:195
  2112.2 54.2 %all-gather.4 = f32[256,1,12]{2,1,0:T(1,128)S(1)} all-gather(f32[1,1,12]{2,1,0:T(1,128)S(1)} %reshape.438), channel_id=1, replica_groups=mesh['group'=16,'member'=16] {'group','member'}, dimensions={0}, use_global_device_ids=true | all-gather | bytes 12336 | tf_op jit(solution)/shard_map/all_gather | solution.py:198
  (781 shorter events, 819.0 us)
Async XLA Ops:
  138.7 190.5 %collective-permute-start = (f32[1,2,256]{2,1,0:T(2,128)S(1)}, f32[1,2,256]{2,1,0:T(2,128)S(1)}, u32[]{:S(2)}, u32[]{:S(2)}) collective-permute-start(f32[1,2,256]{2,1,0:T(2,128)S(1)} %bitcast.922), channel_id=1, source_target_pairs={{0,16},{16,32},{32,48},{48,64},{64,80},{80,96},{96,112},{112,128},... | collective-permute-start | bytes 6152 | tf_op jit(solution)/shard_map/ppermute | solution.py:25
  143.2 186.0 %collective-permute-start.1 = (f32[1,2,256]{2,1,0:T(2,128)S(1)}, f32[1,2,256]{2,1,0:T(2,128)S(1)}, u32[]{:S(2)}, u32[]{:S(2)}) collective-permute-start(f32[1,2,256]{2,1,0:T(2,128)S(1)} %bitcast.923), channel_id=1, source_target_pairs={{16,0},{32,16},{48,32},{64,48},{80,64},{96,80},{112,96},{128,112},... | collective-permute-start | bytes 6152 | tf_op jit(solution)/shard_map/ppermute | solution.py:26
  145.2 192.7 %collective-permute-start.4 = (f32[2,768]{1,0:T(2,128)S(1)}, f32[2,768]{1,0:T(2,128)S(1)}, u32[]{:S(2)}, u32[]{:S(2)}) collective-permute-start(f32[2,768]{1,0:T(2,128)S(1)} %get-tuple-element.600), channel_id=1, source_target_pairs={{0,8},{1,9},{2,10},{3,11},{4,12},{5,13},{6,14},{7,15},{8,0},{9,1},... | collective-permute-start | bytes 18440 | tf_op jit(solution)/shard_map/ppermute | solution.py:15
  152.5 525.3 %collective-permute-start.5 = (f32[768,768]{1,0:T(8,128)}, f32[768,768]{1,0:T(8,128)}, u32[]{:S(2)}, u32[]{:S(2)}) collective-permute-start(f32[768,768]{1,0:T(8,128)} %get-tuple-element.1222), channel_id=1, source_target_pairs={{0,8},{1,9},{2,10},{3,11},{4,12},{5,13},{6,14},{7,15},{8,0},{9,1},... | collective-permute-start | bytes 7077896 | tf_op jit(solution)/shard_map/ppermute | solution.py:15
  681.2 621.6 %collective-permute-start.6 = (f32[768,768]{0,1:T(8,128)}, f32[768,768]{0,1:T(8,128)}, u32[]{:S(2)}, u32[]{:S(2)}) collective-permute-start(f32[768,768]{0,1:T(8,128)} %get-tuple-element.317), channel_id=1, source_target_pairs={{0,8},{1,9},{2,10},{3,11},{4,12},{5,13},{6,14},{7,15},{8,0},{9,1},... | collective-permute-start | bytes 7077896 | tf_op jit(solution)/shard_map/ppermute | solution.py:15
  1311.9 6.4 collective-permute-start.8
  1318.4 12.8 collective-permute-start.9
  1320.3 11.6 collective-permute-start.10
  1479.1 6.1 collective-permute-start.11
  1483.2 6.4 collective-permute-start.12
  1505.3 6.4 collective-permute-start.16
  1657.4 6.6 collective-permute-start.19
  1662.0 6.4 collective-permute-start.20
  1758.8 5.7 collective-permute-start.23
  1762.5 6.4 collective-permute-start.24
  1913.9 6.3 collective-permute-start.27
  1918.2 6.4 collective-permute-start.28
  1924.7 6.1 collective-permute-start.29
  2015.1 5.7 collective-permute-start.31
  2018.8 6.4 collective-permute-start.32
  2025.2 6.2 collective-permute-start.33
  2170.0 6.9 collective-permute-start.35
  2174.3 6.4 collective-permute-start.36
  2180.7 7.0 collective-permute-start.37
  (24 other events, 702.8 us)
where the time goes:
time: 2200 us; the launch traced here: 2190 us
  other arithmetic  759 us (34%)
  blocking collectives  738 us (34%)
  local copies, waits for them, and re-layouts  288 us (13%)
  starting transfers between devices  200 us (9%)
  matrix products  122 us (6%)
  waiting for transfers between devices  54.6 us (2%)
    another operation x48, other arithmetic, lower_solve(): lax.linalg.triangular_solve(panel_matrix, right_side, left_side=True, low...  616 us
    psum x5, blocking collectives, global_sum(): return lax.psum(partial_value, ('group', 'member'))  375 us
    all_gather x5, blocking collectives, gather_coarse(): lax.all_gather(local_coarse.reshape(1, -1), ('group', 'member'), axis=0,...  364 us
    another operation x192, local copies, waits for them, and re-layouts, lower_solve(): lax.linalg.triangular_solve(panel_matrix, right_side, left_side=True, low...  155 us
    another operation x12, other arithmetic, upper_solve(): lax.linalg.triangular_solve(panel_matrix, right_side, left_side=True, low...  123 us
    ppermute x3, starting transfers between devices, from_partner(): return lax.ppermute(value, axis, pairs)  90.3 us
    gather x3, local copies, waits for them, and re-layouts, shards(): jnp.take_along_axis(mode_table, jnp.broadcast_to(dof_map[0][:, None, :],...  71.1 us
    ppermute x18, starting transfers between devices, padded(): before = lax.ppermute(last, axis, up)  63.6 us
  transfers between devices with their start and end apart: 39, of which 17 were waited for; matrix products, arithmetic and copies ran while one was open for 47% of the time, Pallas kernels for 0%

commit v1 on v0

--- a/solution.py
+++ b/solution.py
@@ -195,7 +195,15 @@
         return lax.psum(partial_value, ("group", "member"))
 
     def gather_coarse(local_coarse):
-        return lax.all_gather(local_coarse.reshape(1, -1), ("group", "member"), axis=0, tiled=True)
+        return jnp.concatenate(
+            lax.all_to_all(
+                jnp.stack([local_coarse.reshape(1, -1)] * lax.axis_size(("group", "member"))),
+                ("group", "member"),
+                0,
+                0,
+            ),
+            axis=0,
+        )
 
     def coarse_of(values):
         return jnp.einsum("laj,lj->la", rigid_rows, values, precision=highest)

time: 2200 us -> 1950 us (0.89)
  blocking collectives: 738 us -> 407 us
  starting transfers between devices: 200 us -> 253 us
    all_gather x5 -> x0, blocking collectives: 364 us -> none  [gather_coarse(): lax.all_gather(local_coarse.reshape(1, -1), ('group', 'member'), axis=0,...]
    ppermute x18, starting transfers between devices: 46.3 us -> 138 us  [padded(): after = lax.ppermute(leading, axis, down)]
    ppermute x3, starting transfers between devices: 90.3 us -> 7.51 us  [from_partner(): return lax.ppermute(value, axis, pairs)]
    all_to_all x0 -> x2, blocking collectives: none -> 41.2 us  [gather_coarse(): lax.all_to_all(jnp.stack([local_coarse.reshape(1, -1)] * lax.axis_size(('...]
    all_to_all x0 -> x3, starting transfers between devices: none -> 34.7 us  [gather_coarse(): lax.all_to_all(jnp.stack([local_coarse.reshape(1, -1)] * lax.axis_size(('...]
  transfers between devices with their start and end apart: 39 -> 42, of which waited for: 17 -> 20; matrix products, arithmetic and copies ran while one was open for 47% -> 58% of each run, Pallas kernels for 0% -> 0%
where the time goes in v1:
time: 1950 us; the launch traced here: 1940 us
  other arithmetic  765 us (39%)
  blocking collectives  407 us (21%)
  local copies, waits for them, and re-layouts  291 us (15%)
  starting transfers between devices  253 us (13%)
  matrix products  122 us (6%)
  waiting for transfers between devices  76.5 us (4%)
    another operation x48, other arithmetic, lower_solve(): lax.linalg.triangular_solve(panel_matrix, right_side, left_side=True, low...  616 us
    psum x5, blocking collectives, global_sum(): return lax.psum(partial_value, ('group', 'member'))  366 us
    another operation x192, local copies, waits for them, and re-layouts, lower_solve(): lax.linalg.triangular_solve(panel_matrix, right_side, left_side=True, low...  157 us
    ppermute x18, starting transfers between devices, padded(): after = lax.ppermute(leading, axis, down)  138 us
    another operation x12, other arithmetic, upper_solve(): lax.linalg.triangular_solve(panel_matrix, right_side, left_side=True, low...  123 us
    ppermute x18, starting transfers between devices, padded(): before = lax.ppermute(last, axis, up)  72.6 us
    gather x3, local copies, waits for them, and re-layouts, shards(): jnp.take_along_axis(mode_table, jnp.broadcast_to(dof_map[0][:, None, :],...  71.1 us
    ppermute x18, waiting for transfers between devices, padded(): after = lax.ppermute(leading, axis, down)  57.6 us
  transfers between devices with their start and end apart: 42, of which 20 were waited for; matrix products, arithmetic and copies ran while one was open for 58% of the time, Pallas kernels for 0%

profile of v1, /device:TPU:15, one launch (start us, length us, event | category | flops | bytes accessed | tf_op | source)
XLA Modules:
  0.0 1942.8 jit_solution(9692408481388661312)
XLA Ops:
  30.7 71.1 %gather_fusion = f32[9216]{0:T(1024)S(1)} fusion(f32[2,6,768]{2,1,0:T(8,128)S(1)} %stack.159, s32[9216]{0:T(1024)S(1)} %reshape.398), kind=kCustom, calls=%fused_computation | custom fusion | bytes 184320 | tf_op jit(solution)/shard_map/jit(take_along_axis)/gather | solution.py:158
  125.4 117.9 %custom-call.8 = f32[2,6,128,128]{2,3,1,0:T(8,128)S(1)} custom-call(f32[2,6,128,128]{3,2,1,0:T(8,128)S(1)} %bitcast.1018), custom_call_target="InvertDiagBlocksLowerTriangular" | custom-call | tf_op jit(solution)/shard_map/vmap()/triangular_solve | solution.py:60
  289.4 331.0 %while.88 = (s32[]{:T(128)}, f32[768,768]{1,0:T(8,128)}, s32[]{:T(128)}, f32[768]{0:T(1024)}, f32[768,768]{1,0:T(8,128)}, /*index=5*/s32[]{:T(128)}, s32[]{:T(128)}, s32[]{:T(128)}, s32[]{:T(128)}, s32[]{:T(128)}) while((s32[]{:T(128)}, f32[768,768]{1,0:T(8,128)}, s32[]{:T(128)}, f32[768]{0:T(1024)}, f32[768,768]{1,0:T(8,128)}, ...), condition=%wide.region_12.14_spmd.clone, body=%wide.region_11.13_spmd.clone.sunk | while | flops 530268544 | bytes 10424716 | solution.py:78
  308.3 59.8 %custom-call.57 = f32[6,128,128]{1,2,0:T(8,128)S(1)} custom-call(f32[6,128,128]{2,1,0:T(8,128)} %get-tuple-element.1070), custom_call_target="InvertDiagBlocksLowerTriangular" | custom-call | tf_op jit(solution)/shard_map/while/body/triangular_solve/custom-call.1 | solution.py:56
  391.0 59.8 %custom-call.57 = f32[6,128,128]{1,2,0:T(8,128)S(1)} custom-call(f32[6,128,128]{2,1,0:T(8,128)} %get-tuple-element.1070), custom_call_target="InvertDiagBlocksLowerTriangular" | custom-call | tf_op jit(solution)/shard_map/while/body/triangular_solve/custom-call.1 | solution.py:56
  473.7 59.8 %custom-call.57 = f32[6,128,128]{1,2,0:T(8,128)S(1)} custom-call(f32[6,128,128]{2,1,0:T(8,128)} %get-tuple-element.1070), custom_call_target="InvertDiagBlocksLowerTriangular" | custom-call | tf_op jit(solution)/shard_map/while/body/triangular_solve/custom-call.1 | solution.py:56
  556.4 59.8 %custom-call.57 = f32[6,128,128]{1,2,0:T(8,128)S(1)} custom-call(f32[6,128,128]{2,1,0:T(8,128)} %get-tuple-element.1070), custom_call_target="InvertDiagBlocksLowerTriangular" | custom-call | tf_op jit(solution)/shard_map/while/body/triangular_solve/custom-call.1 | solution.py:56
  622.0 498.4 %while.84 = (s32[]{:T(128)}, f32[768,768]{1,0:T(8,128)}, s32[]{:T(128)}, f32[768]{0:T(1024)}, f32[768,768]{1,0:T(8,128)}, /*index=5*/s32[]{:T(128)}, s32[]{:T(128)}, s32[]{:T(128)}, s32[]{:T(128)}, s32[]{:T(128)}) while((s32[]{:T(128)}, f32[768,768]{1,0:T(8,128)}, s32[]{:T(128)}, f32[768]{0:T(1024)}, f32[768,768]{1,0:T(8,128)}, ...), condition=%wide.region_2.4_spmd.clone, body=%wide.region_1.3_spmd.clone.sunk | while | flops 530268544 | bytes 10424716 | solution.py:78
  641.0 59.8 %custom-call.51 = f32[6,128,128]{1,2,0:T(8,128)S(1)} custom-call(f32[6,128,128]{2,1,0:T(8,128)} %get-tuple-element.1024), custom_call_target="InvertDiagBlocksLowerTriangular" | custom-call | tf_op jit(solution)/shard_map/while/body/triangular_solve/custom-call.1 | solution.py:56
  723.9 59.8 %custom-call.51 = f32[6,128,128]{1,2,0:T(8,128)S(1)} custom-call(f32[6,128,128]{2,1,0:T(8,128)} %get-tuple-element.1024), custom_call_target="InvertDiagBlocksLowerTriangular" | custom-call | tf_op jit(solution)/shard_map/while/body/triangular_solve/custom-call.1 | solution.py:56
  806.9 59.8 %custom-call.51 = f32[6,128,128]{1,2,0:T(8,128)S(1)} custom-call(f32[6,128,128]{2,1,0:T(8,128)} %get-tuple-element.1024), custom_call_target="InvertDiagBlocksLowerTriangular" | custom-call | tf_op jit(solution)/shard_map/while/body/triangular_solve/custom-call.1 | solution.py:56
  889.9 59.8 %custom-call.51 = f32[6,128,128]{1,2,0:T(8,128)S(1)} custom-call(f32[6,128,128]{2,1,0:T(8,128)} %get-tuple-element.1024), custom_call_target="InvertDiagBlocksLowerTriangular" | custom-call | tf_op jit(solution)/shard_map/while/body/triangular_solve/custom-call.1 | solution.py:56
  972.9 59.8 %custom-call.51 = f32[6,128,128]{1,2,0:T(8,128)S(1)} custom-call(f32[6,128,128]{2,1,0:T(8,128)} %get-tuple-element.1024), custom_call_target="InvertDiagBlocksLowerTriangular" | custom-call | tf_op jit(solution)/shard_map/while/body/triangular_solve/custom-call.1 | solution.py:56
  1055.8 59.8 %custom-call.51 = f32[6,128,128]{1,2,0:T(8,128)S(1)} custom-call(f32[6,128,128]{2,1,0:T(8,128)} %get-tuple-element.1024), custom_call_target="InvertDiagBlocksLowerTriangular" | custom-call | tf_op jit(solution)/shard_map/while/body/triangular_solve/custom-call.1 | solution.py:56
  1135.6 23.8 %while.79 = (s32[]{:T(128)}, f32[768,768]{0,1:T(8,128)S(1)}, s32[]{:T(128)}, f32[768,768]{1,0:T(8,128)}, s32[]{:T(128)}, /*index=5*/s32[]{:T(128)}, s32[]{:T(128)}, s32[]{:T(128)}) while((s32[]{:T(128)}, f32[768,768]{0,1:T(8,128)S(1)}, s32[]{:T(128)}, f32[768,768]{1,0:T(8,128)}, s32[]{:T(128)}, /*index=5*/s32[]{:T(128)}, s32[]{:T(128)}, ...), condition=%wide.region_4.6_spmd, body=%wide.region_3.5_spmd.sunk | while | flops 905969664 | bytes 3146883 | solution.py:93
  1184.3 84.4 %collective-permute-start.3 = (f32[3,1,256]{2,1,0:T(1,128)S(1)}, f32[3,1,256]{2,1,0:T(1,128)S(1)}, u32[]{:S(2)}, u32[]{:S(2)}) collective-permute-start(f32[3,1,256]{2,1,0:T(1,128)S(1)} %get-tuple-element.619), channel_id=1, source_target_pairs={{1,0},{2,1},{3,2},{4,3},{5,4},{6,5},{7,6},{8,7},{9,8},{10,9},{11,1... | collective-permute-start | bytes 9224 | tf_op jit(solution)/shard_map/ppermute | solution.py:26
  1286.5 19.8 %collective-permute-start.10 = (f32[3,1,256]{2,1,0:T(1,128)S(1)}, f32[3,1,256]{2,1,0:T(1,128)S(1)}, u32[]{:S(2)}, u32[]{:S(2)}) collective-permute-start(f32[3,1,256]{2,1,0:T(1,128)S(1)} %get-tuple-element.617), channel_id=1, source_target_pairs={{1,0},{2,1},{3,2},{4,3},{5,4},{6,5},{7,6},{8,7},{9,8},{10,9},{11,1... | collective-permute-start | bytes 9224 | tf_op jit(solution)/shard_map/ppermute | solution.py:26
  1376.0 73.2 %all-reduce = (f32[]{:T(128)}, f32[]{:T(128)}) all-reduce(f32[]{:T(128)} %get-tuple-element.439, f32[]{:T(128)} %get-tuple-element.438), channel_id=1, replica_groups=mesh['group'=16,'member'=16] {'group','member'}, use_global_device_ids=true, to_apply=%region_16.18 | all-reduce | flops 2 | bytes 16 | tf_op jit(solution)/shard_map/psum | solution.py:195
  1450.9 20.6 %all_to_all.25 = f32[256,1,12]{2,1,0:T(1,128)S(1)} all-to-all(f32[256,1,12]{2,1,0:T(1,128)S(1)} %stack.185), channel_id=1, replica_groups=mesh['group'=16,'member'=16] {'group','member'}, dimensions={0} | all-to-all | bytes 24576 | tf_op jit(solution)/shard_map/all_to_all | solution.py:199
  1496.9 72.6 %psum.44 = f32[]{:T(128)} all-reduce(f32[]{:T(128)} %fusion.217), channel_id=1, replica_groups=mesh['group'=16,'member'=16] {'group','member'}, use_global_device_ids=true, to_apply=%region_20.22 | all-reduce | flops 1 | bytes 8 | tf_op jit(solution)/shard_map/psum | solution.py:195
  1598.0 73.6 %psum.45 = f32[]{:T(128)} all-reduce(f32[]{:T(128)} %multiply_reduce_fusion.1), channel_id=1, replica_groups=mesh['group'=16,'member'=16] {'group','member'}, use_global_device_ids=true, to_apply=%region_22.24 | all-reduce | flops 1 | bytes 8 | tf_op jit(solution)/shard_map/psum | solution.py:195
  1673.3 20.6 %all_to_all.26 = f32[256,1,12]{2,1,0:T(1,128)S(1)} all-to-all(f32[256,1,12]{2,1,0:T(1,128)S(1)} %stack.192), channel_id=1, replica_groups=mesh['group'=16,'member'=16] {'group','member'}, dimensions={0} | all-to-all | bytes 24576 | tf_op jit(solution)/shard_map/all_to_all | solution.py:199
  1719.2 72.6 %psum.46 = f32[]{:T(128)} all-reduce(f32[]{:T(128)} %get-tuple-element.530), channel_id=1, replica_groups=mesh['group'=16,'member'=16] {'group','member'}, use_global_device_ids=true, to_apply=%region_24.26 | all-reduce | flops 1 | bytes 8 | tf_op jit(solution)/shard_map/psum | solution.py:195
  1820.4 73.6 %psum.47 = f32[]{:T(128)} all-reduce(f32[]{:T(128)} %multiply_reduce_fusion), channel_id=1, replica_groups=mesh['group'=16,'member'=16] {'group','member'}, use_global_device_ids=true, to_apply=%region_26.28 | all-reduce | flops 1 | bytes 8 | tf_op jit(solution)/shard_map/psum | solution.py:195
  (801 shorter events, 806.1 us)
Async XLA Ops:
  1.5 274.6 %collective-permute-start.4 = (f32[2,768]{1,0:T(2,128)S(1)}, f32[2,768]{1,0:T(2,128)S(1)}, u32[]{:S(2)}, u32[]{:S(2)}) collective-permute-start(f32[2,768]{1,0:T(2,128)S(1)} %get-tuple-element.600), channel_id=1, source_target_pairs={{0,8},{1,9},{2,10},{3,11},{4,12},{5,13},{6,14},{7,15},{8,0},{9,1},... | collective-permute-start | bytes 18440 | tf_op jit(solution)/shard_map/ppermute | solution.py:15
  13.3 1151.4 %collective-permute-start.5 = (f32[768,768]{1,0:T(8,128)}, f32[768,768]{1,0:T(8,128)}, u32[]{:S(2)}, u32[]{:S(2)}) collective-permute-start(f32[768,768]{1,0:T(8,128)} %get-tuple-element.1222), channel_id=1, source_target_pairs={{0,8},{1,9},{2,10},{3,11},{4,12},{5,13},{6,14},{7,15},{8,0},{9,1},... | collective-permute-start | bytes 7077896 | tf_op jit(solution)/shard_map/ppermute | solution.py:15
  15.3 1146.1 %all-to-all-start = ((f32[256,1,12]{2,1,0:T(1,128)}), f32[256,1,12]{2,1,0:T(1,128)S(1)}, u32[]{:S(2)}, u32[]{:S(2)}) async-start(f32[256,1,12]{2,1,0:T(1,128)} %stack.160), calls=%async_computation | async-start | bytes 262144 | tf_op jit(solution)/shard_map/all_to_all | solution.py:199
  1166.6 103.8 %collective-permute-start.6 = (f32[768,768]{0,1:T(8,128)S(1)}, f32[768,768]{0,1:T(8,128)S(1)}, u32[]{:S(2)}, u32[]{:S(2)}) collective-permute-start(f32[768,768]{0,1:T(8,128)S(1)} %get-tuple-element.317), channel_id=1, source_target_pairs={{0,8},{1,9},{2,10},{3,11},{4,12},{5,13},{6,14},{7,15},{8,0},{9,1},... | collective-permute-start | bytes 7077896 | tf_op jit(solution)/shard_map/ppermute | solution.py:15
  1168.1 9.5 collective-permute-start
  1175.6 6.7 collective-permute-start.1
  1182.3 86.5 %collective-permute-start.2 = (f32[3,1,256]{2,1,0:T(1,128)S(1)}, f32[3,1,256]{2,1,0:T(1,128)S(1)}, u32[]{:S(2)}, u32[]{:S(2)}) collective-permute-start(f32[3,1,256]{2,1,0:T(1,128)S(1)} %get-tuple-element.618), channel_id=1, source_target_pairs={{0,1},{1,2},{2,3},{3,4},{4,5},{5,6},{6,7},{7,8},{8,9},{9,10},{10,1... | collective-permute-start | bytes 9224 | tf_op jit(solution)/shard_map/ppermute | solution.py:25
  1184.3 85.2 %collective-permute-start.3 = (f32[3,1,256]{2,1,0:T(1,128)S(1)}, f32[3,1,256]{2,1,0:T(1,128)S(1)}, u32[]{:S(2)}, u32[]{:S(2)}) collective-permute-start(f32[3,1,256]{2,1,0:T(1,128)S(1)} %get-tuple-element.619), channel_id=1, source_target_pairs={{1,0},{2,1},{3,2},{4,3},{5,4},{6,5},{7,6},{8,7},{9,8},{10,9},{11,1... | collective-permute-start | bytes 9224 | tf_op jit(solution)/shard_map/ppermute | solution.py:26
  1278.1 6.4 collective-permute-start.8
  1284.6 21.8 %collective-permute-start.9 = (f32[3,1,256]{2,1,0:T(1,128)S(1)}, f32[3,1,256]{2,1,0:T(1,128)S(1)}, u32[]{:S(2)}, u32[]{:S(2)}) collective-permute-start(f32[3,1,256]{2,1,0:T(1,128)S(1)} %get-tuple-element.616), channel_id=1, source_target_pairs={{0,1},{1,2},{2,3},{3,4},{4,5},{5,6},{6,7},{7,8},{8,9},{9,10},{10,1... | collective-permute-start | bytes 9224 | tf_op jit(solution)/shard_map/ppermute | solution.py:25
  1286.5 20.6 %collective-permute-start.10 = (f32[3,1,256]{2,1,0:T(1,128)S(1)}, f32[3,1,256]{2,1,0:T(1,128)S(1)}, u32[]{:S(2)}, u32[]{:S(2)}) collective-permute-start(f32[3,1,256]{2,1,0:T(1,128)S(1)} %get-tuple-element.617), channel_id=1, source_target_pairs={{1,0},{2,1},{3,2},{4,3},{5,4},{6,5},{7,6},{8,7},{9,8},{10,9},{11,1... | collective-permute-start | bytes 9224 | tf_op jit(solution)/shard_map/ppermute | solution.py:26
  1308.9 19.3 all-to-all-start.1
  1335.9 6.4 collective-permute-start.12
  1342.4 7.1 collective-permute-start.13
  1360.0 6.4 collective-permute-start.16
  1479.3 6.4 collective-permute-start.20
  1485.7 6.9 collective-permute-start.21
  1579.6 6.4 collective-permute-start.24
  1586.0 7.7 collective-permute-start.25
  1701.6 6.4 collective-permute-start.28
  1708.1 6.9 collective-permute-start.29
  1808.4 7.7 collective-permute-start.33
  1896.4 20.7 %all-to-all-start.4 = ((f32[256,1,12]{2,1,0:T(1,128)}), f32[256,1,12]{2,1,0:T(1,128)S(1)}, u32[]{:S(2)}, u32[]{:S(2)}) async-start(f32[256,1,12]{2,1,0:T(1,128)} %stack.199), calls=%async_computation.4 | async-start | bytes 262144 | tf_op jit(solution)/shard_map/all_to_all | solution.py:199
  1931.3 6.9 collective-permute-start.37
  (33 other events, 336.5 us)
